TPU v7x, 32 devices: a whole 2x2x4 slice. The times are simulated.
32 devices in a mesh: grp: 2 (over y), inner: 8 (over z, x), outer: 2 (over core).
Axes of the slice: x: 2, y: 2, z: 4, core: 2. Of those that a mesh axis runs over, the one named last changes fastest.
Arguments:
- tokens: bfloat16 [4, 6144, 4096], P(('grp', 'outer'), 'inner'), parts along dimension 0, may hold values from -6 to 6
- w_in: bfloat16 [4096, 1536], P('inner'), may hold values from -0.09375 to 0.09375
- w_dt: bfloat16 [4096, 16], P('inner'), may hold values from -0.09375 to 0.09375
- conv_w: float32 [4, 1536], replicated, may hold values from -0.6 to 0.6
- conv_b: float32 [1536], replicated, may hold values from -0.5 to 0.5
- dt_bias: float32 [16], replicated, may hold values from -2 to 0
- a_log: float32 [16], replicated
- d_skip: float32 [16], replicated, may hold values from 0.5 to 8
- norm_gain: float32 [1024], replicated, may hold values from 0.1 to 1.9
Outputs:
- mixed: bfloat16 [4, 6144, 1024], P(('grp', 'outer'), 'inner'), parts along dimension 0
- entry_states: float32 [4, 8, 16, 64, 256], P(('grp', 'outer'), 'inner'), parts along dimension 0
There are 2 independent parts, one for each index of `grp`. A program takes and returns all parts, laid end to end along the dimension named above; an argument that names none is the same for every part. Nothing has to cross between parts.
All inputs are finite; a program needn't handle non-finite values.
Results may differ from a plain program's by a relative error of at most 0.004.
Values may be sent and summed in bfloat16 or wider, within the bound.
A program may use at most 192 MiB of HBM per device.

v0:
```python
from functools import partial

import jax
import jax.numpy as jnp
from jax import lax
from jax.sharding import PartitionSpec as P

HEADS = 16
P_SIZE = 64
N = 256
CONV = 4


EPSILON = 1e-05


def passed_along(array, axis, by):
    devices = lax.axis_size(axis)
    return lax.ppermute(array, axis, [(i, (i + by) % devices) for i in range(devices)])


def passed_along_2(value, axis, steps):
    count = lax.axis_size(axis)
    leading, last = (max(0, -steps), min(count, count - steps))
    return lax.ppermute(value, axis, [(source, source + steps) for source in range(leading, last)])


def prefix_2(array, axis, combine, identity):
    devices, index = (lax.axis_size(axis), lax.axis_index(axis))
    everything = jax.tree.map(lambda part: lax.all_gather(part, axis), array)
    start = jax.tree.map(
        lambda part, zero: jnp.broadcast_to(jnp.asarray(zero, part.dtype), part.shape),
        array,
        identity,
    )

    def turn(k, before):
        reached = k < index
        new = combine(before, jax.tree.map(lambda part: part[k], everything))
        return jax.tree.map(lambda a, b: jnp.where(reached, a, b), new, before)

    return lax.fori_loop(0, devices, turn, start)


def spread(block, axis, holder):
    block = jnp.where(lax.axis_index(axis) == holder, block, jnp.zeros_like(block))
    return lax.psum(block, axis)


def combine(earlier, later):
    return (earlier[0] * later[0], later[0][:, None, None] * earlier[1] + later[1])


def prepare_span(projected, dt_raw, tail_rows, conv_w, conv_b, dt_bias, a_log):
    length = projected.shape[0]
    padded = jnp.concatenate([tail_rows, projected], axis=0).astype(jnp.float32)
    conv_sum = conv_b[None, :] + conv_w[0][None, :] * padded[0:length]
    for offset in range(1, CONV):
        conv_sum = conv_sum + conv_w[offset][None, :] * padded[offset : offset + length]
    conv_out = jax.nn.silu(conv_sum).astype(jnp.bfloat16)
    inputs = conv_out[:, : HEADS * P_SIZE].reshape(length, HEADS, P_SIZE).transpose(1, 0, 2)
    b_rows = conv_out[:, HEADS * P_SIZE : HEADS * P_SIZE + N]
    c_rows = conv_out[:, HEADS * P_SIZE + N :]
    step_size = jax.nn.softplus(dt_raw.astype(jnp.float32) + dt_bias[None, :]).T
    log_decay = jnp.cumsum(step_size * (-jnp.exp(a_log))[:, None], axis=1)
    return (inputs, b_rows, c_rows, step_size, log_decay)


def span_state(inputs, b_rows, step_size, log_decay):
    final_log = log_decay[:, -1:]
    weighted = (
        (jnp.exp(final_log - log_decay) * step_size)[:, :, None] * inputs.astype(jnp.float32)
    ).astype(jnp.bfloat16)
    contrib = jnp.einsum("hqp,qn->hpn", weighted, b_rows, preferred_element_type=jnp.float32)
    return (jnp.exp(log_decay[:, -1]), contrib)


def head_rows(c_rows, scores, operands):
    log_h, input_h, step_h, entry_h, skip_h, gain_h = operands
    length = log_h.shape[0]
    row_ids = lax.broadcasted_iota(jnp.int32, (length, length), 0)
    col_ids = lax.broadcasted_iota(jnp.int32, (length, length), 1)
    causal = col_ids <= row_ids
    log_gap = jnp.where(causal, log_h[:, None] - log_h[None, :], 0.0)
    mixing = jnp.where(causal, scores * jnp.exp(log_gap), 0.0).astype(jnp.bfloat16)
    driven = (step_h[:, None] * input_h.astype(jnp.float32)).astype(jnp.bfloat16)
    output = jnp.dot(mixing, driven, preferred_element_type=jnp.float32)
    carried = jnp.dot(c_rows, entry_h.astype(jnp.bfloat16).T, preferred_element_type=jnp.float32)
    output = output + jnp.exp(log_h)[:, None] * carried + skip_h * input_h.astype(jnp.float32)
    inv_rms = lax.rsqrt(jnp.mean(output * output, axis=1, keepdims=True) + EPSILON)
    return output * inv_rms * gain_h[None, :]


def span_output(inputs, b_rows, c_rows, step_size, log_decay, entry_state, d_skip, norm_gain):
    scores = jnp.dot(c_rows, b_rows.T, preferred_element_type=jnp.float32)
    head_gains = norm_gain.reshape(HEADS, P_SIZE)
    per_head = lax.map(
        partial(head_rows, c_rows, scores),
        (log_decay, inputs, step_size, entry_state, d_skip, head_gains),
    )
    return per_head.transpose(1, 0, 2).reshape(inputs.shape[1], HEADS * P_SIZE).astype(jnp.bfloat16)


def per_device(tokens, w_in, w_dt, conv_w, conv_b, dt_bias, a_log, d_skip, norm_gain):
    own_rows = tokens.reshape(tokens.shape[1], tokens.shape[2])
    row_count = own_rows.shape[0]
    sums_x = jnp.dot(
        own_rows,
        lax.all_gather(w_in, "inner", axis=0, tiled=True),
        preferred_element_type=jnp.float32,
    )
    sums_dt = jnp.dot(
        own_rows,
        lax.all_gather(w_dt, "inner", axis=0, tiled=True),
        preferred_element_type=jnp.float32,
    )
    projected = sums_x.astype(jnp.bfloat16)
    dt_raw = sums_dt.astype(jnp.bfloat16)
    tail_rows = projected[row_count - CONV + 1 :]
    before = passed_along(tail_rows, "inner", 1)
    prior_block = passed_along_2(before, "outer", 1)
    tail_in = jnp.where(lax.axis_index("inner") == 0, prior_block, before)
    inputs, b_rows, c_rows, step_size, log_decay = prepare_span(
        projected, dt_raw, tail_in, conv_w, conv_b, dt_bias, a_log
    )
    decay_total, contrib = span_state(inputs, b_rows, step_size, log_decay)
    neutral = (jnp.ones_like(decay_total), jnp.zeros_like(contrib))
    prefix = prefix_2((decay_total, contrib), "inner", combine, neutral)
    inclusive = combine(prefix, (decay_total, contrib))
    block_factor, block_state = (
        spread(inclusive[0], "inner", lax.axis_size("inner") - 1),
        spread(inclusive[1], "inner", lax.axis_size("inner") - 1),
    )
    carried = prefix_2((block_factor, block_state), "outer", combine, neutral)
    entry_state = prefix[0][:, None, None] * carried[1] + prefix[1]
    output = span_output(
        inputs, b_rows, c_rows, step_size, log_decay, entry_state, d_skip, norm_gain
    )
    return (
        output.reshape(1, row_count, HEADS * P_SIZE),
        entry_state.reshape(1, 1, HEADS, P_SIZE, N),
    )


def solution(mesh):
    placed = (
        P(("grp", "outer"), "inner", None),
        P("inner", None),
        P("inner", None),
        P(),
        P(),
        P(),
        P(),
        P(),
        P(),
    )
    return jax.shard_map(
        per_device,
        mesh=mesh,
        in_specs=placed,
        out_specs=(
            P(("grp", "outer"), "inner", None),
            P(("grp", "outer"), "inner", None, None, None),
        ),
        check_vma=False,
    )
```

profile of v0, /device:TPU:1, one launch (start us, length us, event | category | flops | bytes accessed | tf_op | source)
XLA Modules:
  0.0 560.1 jit_solution(3436994355984477032)
XLA Ops:
  7.9 26.5 %all_gather.28 = bf16[4096,16]{0,1:T(8,128)(2,1)S(1)} all-gather(bf16[512,16]{0,1:T(8,128)(2,1)} %param.17), channel_id=1, replica_groups=mesh['grp'=2,'inner'=8,'outer'=2] {'inner'}, dimensions={0}, use_global_device_ids=true | all-gather | bytes 147456 | tf_op jit(solution)/shard_map/all_gather | solution.py:114
  35.1 4.6 compare_select_fusion
  42.0 146.2 %all-gather.7.cloned.1.call-done = bf16[4096,1536]{1,0:T(8,128)(2,1)} async-done(((bf16[512,1536]{1,0:T(8,128)(2,1)}), bf16[4096,1536]{1,0:T(8,128)(2,1)}) %all-gather.7.cloned.1.call-update) | async-done | bytes 12582928 | tf_op jit(solution)/shard_map/all_gather | solution.py:109
  188.2 14.7 %fusion.25 = bf16[768,1536]{1,0:T(8,128)(2,1)S(1)} fusion(bf16[4096,1536]{1,0:T(8,128)(2,1)} %all-gather.7.cloned.1.call-done, bf16[1,768,4096]{2,1,0:T(8,128)(2,1)} %param.15), kind=kOutput, calls=%fused_computation.46 | convolution fusion | flops 9664856064 | bytes 21233664 | tf_op jit(solution)/shard_map/dot_general | solution.py:107
  203.4 4.9 collective-permute-done
  209.6 3.1 collective-permute-done.1
  213.5 3.0 multiply_convert_fusion
  218.1 2.6 copy.21
  220.7 3.0 fusion.28
  225.1 14.2 %all-reduce = f32[128]{0:T(128)S(1)} all-reduce(f32[128]{0:T(128)S(1)} %dynamic-update-slice), channel_id=2, replica_groups=mesh['grp'=2,'inner'=8,'outer'=2] {'inner'}, use_global_device_ids=true, to_apply=%add | all-reduce | flops 128 | bytes 1024
  239.4 105.1 %all-gather.11.cloned.1.call-done = f32[128,64,256]{2,1,0:T(8,128)} async-done(((f32[16,64,256]{2,1,0:T(8,128)}), f32[128,64,256]{2,1,0:T(8,128)}) %all-gather.11.cloned.1.call-update) | async-done | bytes 8388624 | tf_op jit(solution)/shard_map/all_gather | solution.py:30
  344.5 12.1 %while.41 = (s32[]{:T(128)}, f32[16]{0:T(128)S(1)}, f32[16,64,256]{2,1,0:T(8,128)S(1)}, s32[]{:T(128)}, f32[8,16]{1,0:T(8,128)S(1)}, /*index=5*/f32[8,16,64,256]{3,2,1,0:T(8,128)}, s32[]{:T(128)}, s32[]{:T(128)}) while((s32[]{:T(128)}, f32[16]{0:T(128)S(1)}, f32[16,64,256]{2,1,0:T(8,128)S(1)}, s32[]{:T(128)}, ...), condition=%wide.region_3.4_spmd.clone, body=%wide.region_2.3_spmd.clone.sunk | while | flops 1048628 | bytes 3146163 | solution.py:42
  357.9 77.2 %all-reduce.3.cloned.1.call-done = f32[1,16,64,256]{3,2,1,0:T(8,128)} async-done(((f32[1,16,64,256]{3,2,1,0:T(8,128)}), f32[1,16,64,256]{3,2,1,0:T(8,128)}) %all-reduce.3.cloned.1.call-update) | async-done | bytes 1048592 | tf_op jit(solution)/shard_map/psum | solution.py:47
  435.2 3.0 fusion.41
  438.2 15.8 %psum.14 = f32[1,16]{1,0:T(1,128)S(1)} all-reduce(f32[1,16]{1,0:T(1,128)S(1)} %get-tuple-element.362), channel_id=1, replica_groups=mesh['grp'=2,'inner'=8,'outer'=2] {'inner'}, use_global_device_ids=true, to_apply=%region_4.5 | all-reduce | flops 16 | bytes 128 | tf_op jit(solution)/shard_map/psum | solution.py:47
  454.1 6.4 %all-gather.2 = f32[2,1,16]{2,1,0:T(1,128)S(1)} all-gather(f32[1,1,16]{2,1,0:T(1,128)S(1)} %bitcast.112), channel_id=1, replica_groups=mesh['grp'=2,'inner'=8,'outer'=2] {'outer'}, dimensions={0}, use_global_device_ids=true | all-gather | bytes 192 | tf_op jit(solution)/shard_map/all_gather | solution.py:30
  460.4 3.0 while.42
  464.6 86.4 %while.40 = (s32[]{:T(128)}, bf16[16,768,64]{1,2,0:T(8,128)(2,1)}, f32[16,768]{1,0:T(8,128)S(1)}, f32[768,768]{1,0:T(8,128)}, f32[16,768]{1,0:T(8,128)S(1)}, /*i...) while((s32[]{:T(128)}, bf16[16,768,64]{1,2,0:T(8,128)(2,1)}, ...), condition=%wide.region_10.11_spmd, body=%wide.region_8.10_spmd.sunk | while | flops 104792832 | bytes 4015489 | solution.py:97
  464.6 2.2 fusion.60
  486.2 2.2 fusion.60
  513.2 2.2 fusion.60
  524.0 2.2 fusion.60
  534.8 2.2 fusion.60
  551.0 2.6 copy.22
  (195 shorter events, 100.8 us)
Async XLA Ops:
  7.2 181.1 %all-gather.7.cloned.1.call-start = ((), (), s32[]{:S(2)}) async-start(), calls=%async_computation | async-start | bytes 14155776 | tf_op jit(solution)/shard_map/all_gather | solution.py:109
  7.9 336.6 %all-gather.11.cloned.1.call-start = ((), (), s32[]{:S(2)}) async-start(), calls=%async_computation.3 | async-start | bytes 9437184 | tf_op jit(solution)/shard_map/all_gather | solution.py:30
  42.0 167.6 %copy-start.2 = (f32[4,1536]{1,0:T(4,128)S(1)}, f32[4,1536]{1,0:T(4,128)}, u32[]{:S(2)}) copy-start(f32[4,1536]{1,0:T(4,128)} %param.18) | copy-start | bytes 73732
  202.9 5.3 collective-permute-start
  208.2 4.5 collective-permute-start.1
  212.7 0.7 copy-start.3
  216.5 4.2 copy-start
  220.7 3.1 copy-start.6
  223.7 211.4 %all-reduce.3.cloned.1.call-start = ((), (), s32[]{:S(2)}) async-start(), calls=%async_computation.1 | async-start | bytes 2097152 | tf_op jit(solution)/shard_map/psum | solution.py:47
  344.5 12.1 %copy-start.1 = (f32[16,64,256]{2,1,0:T(8,128)S(1)}, f32[16,64,256]{2,1,0:T(8,128)}, u32[]{:S(2)}) copy-start(f32[16,64,256]{2,1,0:T(8,128)} %fusion.28) | copy-start | bytes 3145732
  356.6 78.5 %copy-start.4 = (f32[1024]{0:T(1024)S(1)}, f32[1024]{0:T(1024)}, u32[]{:S(2)}) copy-start(f32[1024]{0:T(1024)} %param.23) | copy-start | bytes 12292
  357.8 102.6 %all-gather.9.cloned.1.call-start = ((), (), s32[]{:S(2)}) async-start(), calls=%async_computation.2 | async-start | bytes 3145728 | tf_op jit(solution)/shard_map/all_gather | solution.py:30
  463.4 1.2 slice-start
  463.4 1.2 copy-start.5
Sparse Core Ops, SparseCore 0:
  10.2 178.0 all-gather.6
  223.8 120.6 all-gather.10
  357.9 77.0 all-reduce.2
  436.4 10.6 all-gather.8
where the time goes:
time: 562 us; the launch traced here: 560 us
  waiting for transfers between devices  337 us (60%)
  matrix products  89.3 us (16%)
  blocking collectives  62.9 us (11%)
  other arithmetic  35.2 us (6%)
  local copies, waits for them, and re-layouts  18.3 us (3%)
  between operations  14.6 us (3%)
    all_gather x1, waiting for transfers between devices, per_device(): lax.all_gather(w_in, 'inner', axis=0, tiled=True)  146 us
    all_gather x2, waiting for transfers between devices, prefix_2(): everything = jax.tree.map(lambda part: lax.all_gather(part, axis), array)  105 us
    psum x1, waiting for transfers between devices, spread(): return lax.psum(block, axis)  77.2 us
    dot_general x16, matrix products, head_rows(): output = jnp.dot(mixing, driven, preferred_element_type=jnp.float32)  35 us
    dot_general x16, matrix products, head_rows(): jnp.dot(c_rows, entry_h.astype(jnp.bfloat16).T, preferred_element_type=jn...  29.1 us
    all_gather x1, blocking collectives, per_device(): lax.all_gather(w_dt, 'inner', axis=0, tiled=True)  26.5 us
    psum x1, blocking collectives, spread(): return lax.psum(block, axis)  15.8 us
    select_n x18, other arithmetic, turn(): return jax.tree.map(lambda a, b: jnp.where(reached, a, b), new, before)  14.8 us
  transfers between devices with their start and end apart: 6, of which 5 were waited for; matrix products, arithmetic and copies ran while one was open for 2% of the time, Pallas kernels for 0%

commit v1 on v0

v1 whole, which is shorter than its diff:
```python
from functools import partial

import jax
import jax.numpy as jnp
from jax import lax
from jax.experimental import pallas as pl
from jax.experimental.pallas import tpu as pltpu
from jax.sharding import PartitionSpec as P

HEADS = 16
P_SIZE = 64
N = 256
CONV = 4
HP = HEADS * P_SIZE
CHUNK = 256
EPSILON = 1e-05
MESH = pl.DeviceIdType.MESH
F32 = jnp.float32
BF16 = jnp.bfloat16
LAST = (((1,), (1,)), ((), ()))
FIRST = (((0,), (0,)), ((), ()))


def expand(values, spread):
    high = values.astype(BF16)
    low = (values - high.astype(F32)).astype(BF16)
    return jnp.dot(high, spread, preferred_element_type=F32) + jnp.dot(
        low, spread, preferred_element_type=F32
    )


def scan_kernel(
    n_in, ndev,
    proj, tail, dt_raw, conv_w, conv_b, dt_bias, a_log, d_skip, gain,
    mixed, entry_out,
    pad, conv, log_s, log_t, step_s, y, states,
    send1, recv1, send2, recv2, dec_send, dec_recv,
    ss1, rs1, ss2, rs2, ssd, rsd,
):
    length = proj.shape[0]
    chunks = length // CHUNK
    rows = HP // ndev
    me = lax.axis_index("outer") * n_in + lax.axis_index("inner")

    def place(g):
        return {"inner": lax.rem(g, n_in), "outer": lax.div(g, n_in)}

    barrier = pltpu.get_barrier_semaphore()

    def greet(k, carry):
        pl.semaphore_signal(
            barrier, inc=1, device_id=place(lax.rem(me + k, ndev)), device_id_type=MESH
        )
        return carry

    lax.fori_loop(1, ndev, greet, 0)

    head_id = lax.broadcasted_iota(jnp.int32, (HEADS, HP), 0)
    col_head = lax.broadcasted_iota(jnp.int32, (HEADS, HP), 1) // P_SIZE
    spread = (head_id == col_head).astype(F32).astype(BF16)

    step_size = jax.nn.softplus(dt_raw[...].astype(F32) + dt_bias[...])
    scaled = step_size * (-jnp.exp(a_log[...]))
    row_id = lax.broadcasted_iota(jnp.int32, (CHUNK, CHUNK), 0)
    col_id = lax.broadcasted_iota(jnp.int32, (CHUNK, CHUNK), 1)
    causal = col_id <= row_id
    lower = causal.astype(F32)
    step_s[...] = step_size
    before = jnp.zeros((1, HEADS), F32)
    for c in range(chunks):
        part = jnp.dot(
            lower,
            scaled[c * CHUNK : (c + 1) * CHUNK],
            preferred_element_type=F32,
            precision=lax.Precision.HIGHEST,
        ) + before
        log_s[c * CHUNK : (c + 1) * CHUNK] = part
        before = part[CHUNK - 1 : CHUNK]
    log_t[...] = jnp.transpose(log_s[...])
    dec_send[...] = jnp.broadcast_to(jnp.exp(log_t[:, length - 1 : length]), (HEADS, 128))

    pad[0:8] = tail[...].astype(F32)
    pad[8:] = proj[...].astype(F32)
    wide = 256
    blocks = proj.shape[1] // wide

    def conv_block(t, carry):
        i, j = lax.div(t, blocks), lax.rem(t, blocks)
        cols = pl.ds(pl.multiple_of(j * wide, wide), wide)
        window = pad[pl.ds(pl.multiple_of(i * 128, 128), 136), cols]
        total = conv_b[:, cols]
        for k in range(CONV):
            total = total + conv_w[k : k + 1, cols] * window[5 + k : 5 + k + 128]
        conv[pl.ds(pl.multiple_of(i * 128, 128), 128), cols] = (
            total * jax.nn.sigmoid(total)
        ).astype(BF16)
        return carry

    lax.fori_loop(0, (length // 128) * blocks, conv_block, 0)

    def weighted_sum(stop):
        final = log_s[stop - 1 : stop]
        factor = jnp.exp(final - log_s[0:stop]) * step_s[0:stop]
        weighted = (expand(factor, spread) * conv[0:stop, 0:HP].astype(F32)).astype(BF16)
        return lax.dot_general(
            weighted, conv[0:stop, HP : HP + N], FIRST, preferred_element_type=F32
        )

    send1[...] = weighted_sum(length).reshape(ndev, rows, N).astype(BF16)
    recv1[me] = send1[me]
    dec_recv[me] = dec_send[...]

    def decay_copy(g):
        return pltpu.make_async_remote_copy(
            src_ref=dec_send, dst_ref=dec_recv.at[me], send_sem=ssd.at[g],
            recv_sem=rsd.at[me], device_id=place(g), device_id_type=MESH,
        )

    def first_copy(g):
        return pltpu.make_async_remote_copy(
            src_ref=send1.at[g], dst_ref=recv1.at[me], send_sem=ss1.at[g],
            recv_sem=rs1.at[me], device_id=place(g), device_id_type=MESH,
        )

    def second_copy(g):
        return pltpu.make_async_remote_copy(
            src_ref=send2.at[g], dst_ref=recv2.at[me], send_sem=ss2.at[g],
            recv_sem=rs2.at[me], device_id=place(g), device_id_type=MESH,
        )

    pl.semaphore_wait(barrier, ndev - 1)

    def send_first(k, carry):
        g = lax.rem(me + k, ndev)
        decay_copy(g).start()
        first_copy(g).start()
        return carry

    lax.fori_loop(1, ndev, send_first, 0)

    states[0] = jnp.zeros((HP, N), BF16)
    for c in range(1, chunks):
        states[c] = weighted_sum(c * CHUNK).astype(BF16)

    def local_chunk(c, carry):
        start = pl.multiple_of(c * CHUNK, CHUNK)
        here = pl.ds(start, CHUNK)
        log_c = log_s[here]
        reached = log_s[pl.ds(pl.multiple_of(jnp.maximum(start - 8, 0), 8), 8)][7:8]
        reached = jnp.where(c > 0, reached, 0.0)
        c_rows = conv[here, HP + N :]
        b_rows = conv[here, HP : HP + N]
        scores = lax.dot_general(c_rows, b_rows, LAST, preferred_element_type=F32)
        scores = jnp.where(causal, scores, 0.0)
        x_rows = conv[here, 0:HP].astype(F32)
        driven = (expand(step_s[here], spread) * x_rows).astype(BF16)
        inter = lax.dot_general(c_rows, states[c], LAST, preferred_element_type=F32)
        y[here] = expand(jnp.exp(log_c - reached), spread) * inter + d_skip[...] * x_rows
        for h in range(0, HEADS, 2):
            pieces = []
            for k in (h, h + 1):
                gap = jnp.minimum(log_c[:, k : k + 1] - log_t[k : k + 1, here], 0.0)
                mixing = (scores * jnp.exp(gap)).astype(BF16)
                pieces.append(
                    jnp.dot(
                        mixing,
                        driven[:, k * P_SIZE : (k + 1) * P_SIZE],
                        preferred_element_type=F32,
                    )
                )
            both = slice(h * P_SIZE, (h + 2) * P_SIZE)
            y[here, both] = y[here, both] + jnp.concatenate(pieces, axis=1)
        return carry

    lax.fori_loop(0, chunks, local_chunk, 0)

    own_head = lax.div(me * rows, P_SIZE)

    def wait_from(copy_of, r):
        copy_of(r).wait_recv()

    def arrive(buffer, sems, r):
        pltpu.make_async_remote_copy(
            src_ref=buffer.at[r], dst_ref=buffer.at[r], send_sem=sems.at[r],
            recv_sem=sems.at[r], device_id=place(r), device_id_type=MESH,
        ).wait_recv()

    def advance(r, state):
        send2[r] = state.astype(BF16)

        @pl.when(r != me)
        def _():
            second_copy(r).start()
            arrive(dec_recv, rsd, r)
            arrive(recv1, rs1, r)

        decay = dec_recv[r, pl.ds(own_head, 1), :]
        decay = jnp.concatenate([decay, decay], axis=1)
        return decay * state + recv1[r].astype(F32)

    lax.fori_loop(0, ndev, advance, jnp.zeros((rows, N), F32))
    recv2[me] = send2[me]

    def finish(k, carry):
        g = lax.rem(me + k, ndev)
        arrive(recv2, rs2, g)
        decay_copy(g).wait_send()
        first_copy(g).wait_send()
        second_copy(g).wait_send()
        return carry

    lax.fori_loop(1, ndev, finish, 0)

    entry = recv2[...].astype(F32).reshape(HP, N)
    entry_out[...] = entry
    entry = entry.astype(BF16)
    for c in range(chunks):
        here = slice(c * CHUNK, (c + 1) * CHUNK)
        carried = lax.dot_general(
            conv[here, HP + N :], entry, LAST, preferred_element_type=F32
        )
        out = y[here] + expand(jnp.exp(log_s[here]), spread) * carried
        square = out * out
        high = square.astype(BF16)
        low = (square - high.astype(F32)).astype(BF16)
        sums = lax.dot_general(high, spread, LAST, preferred_element_type=F32)
        sums = sums + lax.dot_general(low, spread, LAST, preferred_element_type=F32)
        inv_rms = lax.rsqrt(sums * (1.0 / P_SIZE) + EPSILON)
        mixed[here] = (out * expand(inv_rms, spread) * gain[...]).astype(BF16)


def run_scan(projected, tail, dt_raw, conv_w, conv_b, dt_bias, a_log, d_skip, norm_gain):
    n_in, n_out = lax.axis_size("inner"), lax.axis_size("outer")
    ndev = n_in * n_out
    length, xbc = projected.shape
    rows = HP // ndev
    dma = pltpu.SemaphoreType.DMA((ndev,))
    vmem = pl.BlockSpec(memory_space=pltpu.VMEM)
    return pl.pallas_call(
        partial(scan_kernel, n_in, ndev),
        out_shape=(
            jax.ShapeDtypeStruct((length, HP), BF16),
            jax.ShapeDtypeStruct((HP, N), F32),
        ),
        in_specs=[vmem] * 9,
        out_specs=(vmem, vmem),
        scratch_shapes=[
            pltpu.VMEM((length + 8, xbc), F32),
            pltpu.VMEM((length, xbc), BF16),
            pltpu.VMEM((length, HEADS), F32),
            pltpu.VMEM((HEADS, length), F32),
            pltpu.VMEM((length, HEADS), F32),
            pltpu.VMEM((length, HP), F32),
            pltpu.VMEM((length // CHUNK, HP, N), BF16),
            pltpu.VMEM((ndev, rows, N), BF16),
            pltpu.VMEM((ndev, rows, N), BF16),
            pltpu.VMEM((ndev, rows, N), BF16),
            pltpu.VMEM((ndev, rows, N), BF16),
            pltpu.VMEM((HEADS, 128), F32),
            pltpu.VMEM((ndev, HEADS, 128), F32),
            dma, dma, dma, dma, dma, dma,
        ],
        compiler_params=pltpu.CompilerParams(
            collective_id=1, has_side_effects=True, vmem_limit_bytes=60 * 2**20
        ),
        name="scan",
    )(
        projected, tail, dt_raw, conv_w, conv_b[None, :], dt_bias[None, :], a_log[None, :],
        jnp.repeat(d_skip, P_SIZE)[None, :], norm_gain[None, :],
    )


def per_device(tokens, w_in, w_dt, conv_w, conv_b, dt_bias, a_log, d_skip, norm_gain):
    own_rows = tokens.reshape(tokens.shape[1], tokens.shape[2])
    row_count = own_rows.shape[0]
    n_in, n_out = lax.axis_size("inner"), lax.axis_size("outer")
    full_x = lax.all_gather(w_in, "inner", axis=0, tiled=True)
    full_dt = lax.all_gather(w_dt, "inner", axis=0, tiled=True)
    projected = jnp.dot(own_rows, full_x, preferred_element_type=F32).astype(BF16)
    dt_raw = jnp.dot(own_rows, full_dt, preferred_element_type=F32).astype(BF16)
    order = [(r, r + 1) for r in range(n_in * n_out - 1)]
    pairs = [((r % n_in) * n_out + r // n_in, (s % n_in) * n_out + s // n_in) for r, s in order]
    tail = lax.ppermute(projected[row_count - 8 :], ("inner", "outer"), pairs)
    mixed, entry = run_scan(
        projected, tail, dt_raw, conv_w, conv_b, dt_bias, a_log, d_skip, norm_gain
    )
    return (
        mixed.reshape(1, row_count, HP),
        entry.reshape(1, 1, HEADS, P_SIZE, N),
    )


def solution(mesh):
    placed = (
        P(("grp", "outer"), "inner", None),
        P("inner", None),
        P("inner", None),
        P(), P(), P(), P(), P(), P(),
    )
    return jax.shard_map(
        per_device,
        mesh=mesh,
        in_specs=placed,
        out_specs=(
            P(("grp", "outer"), "inner", None),
            P(("grp", "outer"), "inner", None, None, None),
        ),
        check_vma=False,
    )
```

time: 562 us -> 267 us (0.48)
  waiting for transfers between devices: 337 us -> 154 us
  matrix products: 89.3 us -> 19.2 us
  Pallas kernels: 0 us -> 42.4 us
  blocking collectives: 62.9 us -> 26.5 us
  other arithmetic: 35.2 us -> 0 us
  local copies, waits for them, and re-layouts: 18.3 us -> 7.76 us
    all_gather x3 -> x1, waiting for transfers between devices: 251 us -> 154 us  [per_device(): full_x = lax.all_gather(w_in, 'inner', axis=0, tiled=True)]
    psum x1 -> x0, waiting for transfers between devices: 77.2 us -> none  [spread(): return lax.psum(block, axis)]
    dot_general x36 -> x2, matrix products: 89.3 us -> 19.2 us  [the longest x1 14.7 us: per_device(): jnp.dot(own_rows, full_x, preferred_element_type=F32).astype(BF16)]
    pallas_call x0 -> x1, Pallas kernels: none -> 42.4 us  [run_scan(): pl.pallas_call(partial(scan_kernel, n_in, ndev), out_shape=(jax.ShapeDtyp...]
    psum x1 -> x0, blocking collectives: 15.8 us -> none  [spread(): return lax.psum(block, axis)]
    select_n x19 -> x0, other arithmetic: 14.8 us -> none  [the longest x18 14.8 us: turn(): return jax.tree.map(lambda a, b: jnp.where(reached, a, b), new, before)]
    unnamed x1 -> x0, blocking collectives: 14.2 us -> none
    dynamic_update_slice x16 -> x0, other arithmetic: 11.5 us -> none  [span_output(): lax.map(partial(head_rows, c_rows, scores), (log_decay, inputs, step_size...]
  transfers between devices with their start and end apart: 6 -> 2, of which waited for: 5 -> 1; matrix products, arithmetic and copies ran while one was open for 2% -> 3% of each run, Pallas kernels for 0% -> 0%
where the time goes in v1:
time: 267 us
  waiting for transfers between devices  154 us (58%)
  Pallas kernels  42.4 us (16%)
  blocking collectives  26.5 us (10%)
  matrix products  19.2 us (7%)
  between operations  14.1 us (5%)
  local copies, waits for them, and re-layouts  7.76 us (3%)
    all_gather x1, waiting for transfers between devices, per_device(): full_x = lax.all_gather(w_in, 'inner', axis=0, tiled=True)  154 us
    pallas_call x1, Pallas kernels, run_scan(): pl.pallas_call(partial(scan_kernel, n_in, ndev), out_shape=(jax.ShapeDtyp...  42.4 us
    all_gather x1, blocking collectives, per_device(): full_dt = lax.all_gather(w_dt, 'inner', axis=0, tiled=True)  26.5 us
    dot_general x1, matrix products, per_device(): jnp.dot(own_rows, full_x, preferred_element_type=F32).astype(BF16)  14.7 us
    unnamed x10, local copies, waits for them, and re-layouts  5.58 us
  transfers between devices with their start and end apart: 2, of which 1 were waited for; matrix products, arithmetic and copies ran while one was open for 3% of the time, Pallas kernels for 0%

profile of v1, /device:TPU:1, one launch (start us, length us, event | category | flops | bytes accessed | tf_op | source)
XLA Modules:
  0.0 267.0 jit_solution(13822280383032064872)
XLA Ops:
  7.2 0.0 all-gather.2.cloned.1.call-start
  7.2 0.7 all-gather.2.cloned.1.call-update
  7.9 26.5 %all_gather.7 = bf16[4096,16]{0,1:T(8,128)(2,1)S(1)} all-gather(bf16[512,16]{0,1:T(8,128)(2,1)} %param.11), channel_id=1, replica_groups=mesh['grp'=2,'inner'=8,'outer'=2] {'inner'}, dimensions={0}, use_global_device_ids=true | all-gather | bytes 147456 | tf_op jit(solution)/shard_map/all_gather | solution.py:278
  34.4 153.8 %all-gather.2.cloned.1.call-done = bf16[4096,1536]{1,0:T(8,128)(2,1)} async-done(((bf16[512,1536]{1,0:T(8,128)(2,1)}), bf16[4096,1536]{1,0:T(8,128)(2,1)}) %all-gather.2.cloned.1.call-update) | async-done | bytes 12582928 | tf_op jit(solution)/shard_map/all_gather | solution.py:277
  188.2 14.7 %fusion.4.proj = bf16[768,1536]{1,0:T(8,128)(2,1)S(1)} fusion(bf16[4096,1536]{1,0:T(8,128)(2,1)} %all-gather.2.cloned.1.call-done, bf16[1,768,4096]{2,1,0:T(8,128)(2,1)} %param.9), kind=kOutput, calls=%fused_computation.4 | convolution fusion | flops 9664856064 | bytes 21233664 | tf_op jit(solution)/shard_map/dot_general | solution.py:279
  202.9 0.0 copy-start
  202.9 0.0 copy-start.2
  202.9 0.0 copy-start.3
  203.0 2.5 collective-permute-start
  205.5 4.5 %fusion.7 = bf16[768,16]{0,1:T(8,128)(2,1)S(1)} fusion(bf16[4096,16]{0,1:T(8,128)(2,1)S(1)} %all_gather.7, bf16[1,768,4096]{2,1,0:T(8,128)(2,1)} %param.9), kind=kOutput, calls=%fused_computation.5 | convolution fusion | flops 100675584 | bytes 6447104 | tf_op jit(solution)/shard_map/dot_general | solution.py:280
  210.0 0.0 copy-done.2
  210.0 0.6 broadcast_in_dim.15.conv_b
  210.6 0.0 copy-done.3
  210.6 0.1 broadcast_in_dim.18
  210.7 0.7 broadcast_in_dim_reshape.3.d_skip
  211.3 0.8 copy.12.dt_raw
  212.1 0.0 collective-permute-done.tail
  212.2 0.0 copy-start.1
  212.2 0.0 copy-done
  212.2 0.6 copy-done.1
  212.8 42.4 %scan.1 = (bf16[768,1024]{1,0:T(8,128)(2,1)}, f32[1024,256]{1,0:T(8,128)}) custom-call(bf16[768,1536]{1,0:T(8,128)(2,1)} %copy-done, bf16[8,1536]{1,0:T(8,128)(2,1)} %copy-done.1, bf16[768,16]{1,0:T(8,128)(2,1)} %copy.12.dt_raw, f32[4,1536]{1,0:T(4,128)} %conv_w.1, f32[1,1536]{1,0:T(1,128)} %broadcast_in_dim.15.conv_b, f32[1,16]{1,0:T(1,128)} %bitcast.19, ...), custom_call_target="tpu_custom_call" | custom-call | tf_op jit(solution)/shard_map/scan/pallas_call | solution.py:239
  255.2 2.7 copy.15
  257.9 2.3 copy.16
  (1 shorter events, 0.0 us)
Async XLA Ops:
  7.2 181.1 %all-gather.2.cloned.1.call-start = ((), (), s32[]{:S(2)}) async-start(), calls=%async_computation | async-start | bytes 14155776 | tf_op jit(solution)/shard_map/all_gather | solution.py:277
  202.9 9.2 %copy-start = (bf16[768,1536]{1,0:T(8,128)(2,1)}, bf16[768,1536]{1,0:T(8,128)(2,1)S(1)}, u32[]{:S(2)}) copy-start(bf16[768,1536]{1,0:T(8,128)(2,1)S(1)} %fusion.4.proj) | copy-start | bytes 7077892
  202.9 7.1 %copy-start.2 = (f32[1536]{0:T(1024)S(1)}, f32[1536]{0:T(1024)}, u32[]{:S(2)}) copy-start(f32[1536]{0:T(1024)} %param.13) | copy-start | bytes 18436
  202.9 7.7 %copy-start.3 = (f32[16]{0:T(128)S(1)}, f32[16]{0:T(128)}, u32[]{:S(2)}) copy-start(f32[16]{0:T(128)} %param.16) | copy-start | bytes 196
  203.0 9.2 %collective-permute-start = (bf16[8,1536]{1,0:T(8,128)(2,1)S(1)}, bf16[8,1536]{1,0:T(8,128)(2,1)S(1)}, u32[]{:S(2)}, u32[]{:S(2)}) collective-permute-start(bf16[8,1536]{1,0:T(8,128)(2,1)S(1)} %slice.4), channel_id=1, source_target_pairs={{0,2},{2,4},{4,6},{6,8},{8,10},{10,12},{12,14},{14,1},{1,3},{3,5},... | collective-permute-start | bytes 73736 | tf_op jit(solution)/shard_map/ppermute | solution.py:283
  212.2 0.6 copy-start.1
Sparse Core Ops, SparseCore 0:
  10.2 178.0 all-gather.1

commit v2 on v1

--- a/solution.py
+++ b/solution.py
@@ -79,7 +79,7 @@
     log_t[...] = jnp.transpose(log_s[...])
     dec_send[...] = jnp.broadcast_to(jnp.exp(log_t[:, length - 1 : length]), (HEADS, 128))
 
-    pad[0:8] = tail[...].astype(F32)
+    pad[0:8] = tail[...].astype(F32)[8:16]
     pad[8:] = proj[...].astype(F32)
     wide = 256
     blocks = proj.shape[1] // wide
@@ -270,17 +270,335 @@
     )
 
 
+def project_kernel(
+    n, n_out,
+    tokens, w_in, w_dt,
+    proj, tail, dt_out,
+    tok, held, total, held_dt,
+    ring_s, ring_r, side_s, side_r, core_s, core_r, dt_s, dt_r, misc, tail_s, tail_r,
+):
+    length, depth = tokens.shape
+    local, xbc = w_in.shape
+    half = xbc // 2
+    quarter = half // 2
+    lanes = 128
+    streams = quarter // lanes
+    wide = 256
+    tiles = half // wide
+    third = (local * 5 // 16) // 16 * 16
+    ring_rows = local - third
+    tail_rows = tok.shape[0] - length
+    block = held_dt.shape[2]
+    ndev = n * n_out
+    me = lax.axis_index("inner")
+    core = lax.axis_index("outer")
+    grp = lax.axis_index("grp")
+    rank = core * n + me
+    odd = lax.rem(me, 2)
+    pos = jnp.where(odd == 0, lax.div(me, 2), n - lax.div(me + 1, 2))
+
+    def index_at(q):
+        q = lax.rem(q + 2 * n, n)
+        return jnp.where(q < n // 2, 2 * q, 2 * n - 1 - 2 * q)
+
+    def place(g):
+        return {"inner": lax.rem(g, n), "outer": lax.div(g, n)}
+
+    barrier = pltpu.get_barrier_semaphore()
+
+    def greet(k, carry):
+        pl.semaphore_signal(
+            barrier, inc=1, device_id=place(lax.rem(rank + k, ndev)), device_id_type=MESH
+        )
+        return carry
+
+    lax.fori_loop(1, ndev, greet, 0)
+    pl.semaphore_signal(barrier, inc=1, device_id={"grp": 1 - grp}, device_id_type=MESH)
+
+    def own_rows(owner):
+        return pl.ds(pl.multiple_of(owner * local, 16), local)
+
+    load_tok = pltpu.make_async_copy(tokens, tok.at[pl.ds(0, length)], misc.at[0])
+    load_w = [
+        pltpu.make_async_copy(
+            w_in.at[:, pl.ds(d * half, half)], held.at[d, own_rows(me)], misc.at[1 + d]
+        )
+        for d in range(2)
+    ]
+    for copy in load_w:
+        copy.start()
+    load_tok.start()
+    held_dt[me] = w_dt[...]
+
+    @pl.when(rank == 0)
+    def _():
+        tok[length:] = jnp.zeros((tail_rows, depth), BF16)
+
+    def ring_copy(d, t, s):
+        owner = index_at(pos - (s - 1)) if d == 0 else index_at(pos + (s - 1))
+        target = index_at(pos + 1) if d == 0 else index_at(pos - 1)
+        rows = pl.ds(pl.multiple_of(owner * local + grp * third, 16), ring_rows)
+        cols = pl.ds(pl.multiple_of(core * quarter + t * lanes, lanes), lanes)
+        part = held.at[d, rows, cols]
+        return pltpu.make_async_remote_copy(
+            src_ref=part, dst_ref=part, send_sem=ring_s.at[d, t, s],
+            recv_sem=ring_r.at[d, t, s], device_id={"inner": target}, device_id_type=MESH,
+        )
+
+    def owner_of(d, s):
+        return index_at(pos - s) if d == 0 else index_at(pos + s)
+
+    def side_copy(d, s):
+        rows = pl.ds(
+            pl.multiple_of(owner_of(d, s) * local + grp * ring_rows, 16), third
+        )
+        cols = pl.ds(pl.multiple_of(core * quarter, lanes), quarter)
+        part = held.at[d, rows, cols]
+        return pltpu.make_async_remote_copy(
+            src_ref=part, dst_ref=part, send_sem=side_s.at[d, s],
+            recv_sem=side_r.at[d, s], device_id={"grp": 1 - grp}, device_id_type=MESH,
+        )
+
+    def core_copy(d, s):
+        cols = pl.ds(pl.multiple_of(core * quarter, lanes), quarter)
+        part = held.at[d, own_rows(owner_of(d, s)), cols]
+        return pltpu.make_async_remote_copy(
+            src_ref=part, dst_ref=part, send_sem=core_s.at[d, s],
+            recv_sem=core_r.at[d, s], device_id={"outer": 1 - core}, device_id_type=MESH,
+        )
+
+    def ring_arrival(d, t, s):
+        owner = owner_of(d, s)
+        rows = pl.ds(pl.multiple_of(owner * local + grp * third, 16), ring_rows)
+        cols = pl.ds(pl.multiple_of(core * quarter + t * lanes, lanes), lanes)
+        part = held.at[d, rows, cols]
+        pltpu.make_async_remote_copy(
+            src_ref=part, dst_ref=part, send_sem=ring_s.at[d, t, s],
+            recv_sem=ring_r.at[d, t, s], device_id={"inner": index_at(pos + 1)},
+            device_id_type=MESH,
+        ).wait_recv()
+
+    def side_arrival(d, s):
+        rows = pl.ds(
+            pl.multiple_of(owner_of(d, s) * local + (1 - grp) * ring_rows, 16), third
+        )
+        cols = pl.ds(pl.multiple_of(core * quarter, lanes), quarter)
+        part = held.at[d, rows, cols]
+        pltpu.make_async_remote_copy(
+            src_ref=part, dst_ref=part, send_sem=side_s.at[d, s],
+            recv_sem=side_r.at[d, s], device_id={"grp": 1 - grp}, device_id_type=MESH,
+        ).wait_recv()
+
+    def core_arrival(d, s):
+        cols = pl.ds(pl.multiple_of((1 - core) * quarter, lanes), quarter)
+        part = held.at[d, own_rows(owner_of(d, s)), cols]
+        pltpu.make_async_remote_copy(
+            src_ref=part, dst_ref=part, send_sem=core_s.at[d, s],
+            recv_sem=core_r.at[d, s], device_id={"outer": 1 - core}, device_id_type=MESH,
+        ).wait_recv()
+
+    def dt_copy(k):
+        peer = lax.rem(me + k, n)
+        return pltpu.make_async_remote_copy(
+            src_ref=w_dt, dst_ref=held_dt.at[me], send_sem=dt_s.at[k],
+            recv_sem=dt_r.at[me], device_id={"inner": peer}, device_id_type=MESH,
+        )
+
+    def dt_arrival(k):
+        peer = lax.rem(me + k, n)
+        pltpu.make_async_remote_copy(
+            src_ref=w_dt, dst_ref=held_dt.at[peer], send_sem=dt_s.at[k],
+            recv_sem=dt_r.at[peer], device_id={"inner": peer}, device_id_type=MESH,
+        ).wait_recv()
+
+    def tail_copy():
+        return pltpu.make_async_remote_copy(
+            src_ref=tokens.at[pl.ds(length - tail_rows, tail_rows)],
+            dst_ref=tok.at[pl.ds(length, tail_rows)], send_sem=tail_s,
+            recv_sem=tail_r, device_id=place(lax.rem(rank + 1, ndev)), device_id_type=MESH,
+        )
+
+    pl.semaphore_wait(barrier, ndev)
+
+    @pl.when(rank < ndev - 1)
+    def _():
+        tail_copy().start()
+
+    for d in range(2):
+        load_w[d].wait()
+        for t in range(streams):
+            ring_copy(d, t, 1).start()
+
+    def send_dt(k, carry):
+        dt_copy(k).start()
+        return carry
+
+    lax.fori_loop(1, n, send_dt, 0)
+    load_tok.wait()
+
+    @pl.when(rank > 0)
+    def _():
+        tail_copy().wait_recv()
+
+    incremental = local % 128 == 0
+
+    def multiply(d, lhs_cols, rhs_rows, first):
+        def tile(j, carry):
+            cols = pl.ds(pl.multiple_of(j * wide, wide), wide)
+            product = jnp.dot(
+                tok[:, lhs_cols], held[d, rhs_rows, cols], preferred_element_type=F32
+            )
+            at = d * tiles + j
+            if first:
+                total[at] = product
+            else:
+                total[at] = total[at] + product
+            return carry
+
+        lax.fori_loop(0, tiles, tile, 0)
+
+    def project_dt():
+        def arrived(k, carry):
+            dt_arrival(k)
+            return carry
+
+        lax.fori_loop(1, n, arrived, 0)
+        together = block // local
+
+        def add(j, sums):
+            cols = pl.ds(pl.multiple_of(j * block, block), block)
+            piece = held_dt[j * together]
+            for m in range(1, together):
+                piece = piece + held_dt[j * together + m]
+            return sums + lax.dot_general(
+                tok[0:length, cols], piece, LAST, preferred_element_type=F32
+            )
+
+        sums = lax.fori_loop(0, depth // block, add, jnp.zeros((length, HEADS), F32))
+        dt_out[...] = sums.astype(BF16)
+
+    def step(s, carry):
+        @pl.when(s < n)
+        def _():
+            for t in range(streams):
+                for d in range(2):
+                    ring_arrival(d, t, s)
+
+                    @pl.when(s < n - 1)
+                    def _():
+                        ring_copy(d, t, s + 1).start()
+
+            for d in range(2):
+                side_copy(d, s).start()
+
+        @pl.when((s >= 2) & (s <= n))
+        def _():
+            for d in range(2):
+                side_arrival(d, s - 1)
+                core_copy(d, s - 1).start()
+
+        @pl.when(s >= 3)
+        def _():
+            for d in range(2):
+                core_arrival(d, s - 2)
+
+        @pl.when(s == 1)
+        def _():
+            project_dt()
+
+        if incremental:
+            for d in range(2):
+                owner = owner_of(d, s - 2)
+                at = pl.ds(pl.multiple_of(owner * local, 128), local)
+
+                @pl.when(s == 2)
+                def _():
+                    multiply(d, at, at, True)
+
+                @pl.when(s > 2)
+                def _():
+                    multiply(d, at, at, False)
+
+        return carry
+
+    lax.fori_loop(1, n + 2, step, 0)
+    if not incremental:
+        for d in range(2):
+            multiply(d, slice(0, 512), slice(0, 512), True)
+
+            def more(j, carry):
+                at = pl.ds(pl.multiple_of(j * 512, 512), 512)
+                multiply(d, at, at, False)
+                return carry
+
+            lax.fori_loop(1, depth // 512, more, 0)
+
+    for j in range(2 * tiles):
+        cols = slice(j * wide, (j + 1) * wide)
+        proj[:, cols] = total[j, 0:length].astype(BF16)
+        tail[:, cols] = total[j, length:].astype(BF16)
+
+    def drain(s, carry):
+        for d in range(2):
+            for t in range(streams):
+                ring_copy(d, t, s).wait_send()
+            side_copy(d, s).wait_send()
+            core_copy(d, s).wait_send()
+        dt_copy(s).wait_send()
+        return carry
+
+    lax.fori_loop(1, n, drain, 0)
+
+    @pl.when(rank < ndev - 1)
+    def _():
+        tail_copy().wait_send()
+
+
+def run_project(tokens, w_in, w_dt):
+    n, n_out = lax.axis_size("inner"), lax.axis_size("outer")
+    length, depth = tokens.shape
+    local, xbc = w_in.shape
+    block = max(local, 128)
+    tail_rows = 16
+    dt_block = w_dt.T
+    if block != local:
+        start = lax.rem(lax.axis_index("inner") * local, block)
+        dt_block = lax.dynamic_update_slice(
+            jnp.zeros((HEADS, block), BF16), dt_block, (jnp.int32(0), start)
+        )
+    streams = xbc // 4 // 128
+    dma = pltpu.SemaphoreType.DMA
+    vmem = pl.BlockSpec(memory_space=pltpu.VMEM)
+    whole = pl.BlockSpec(memory_space=pl.ANY)
+    return pl.pallas_call(
+        partial(project_kernel, n, n_out),
+        out_shape=(
+            jax.ShapeDtypeStruct((length, xbc), BF16),
+            jax.ShapeDtypeStruct((tail_rows, xbc), BF16),
+            jax.ShapeDtypeStruct((length, HEADS), BF16),
+        ),
+        in_specs=[whole, whole, vmem],
+        out_specs=(vmem, vmem, vmem),
+        scratch_shapes=[
+            pltpu.VMEM((length + tail_rows, depth), BF16),
+            pltpu.VMEM((2, depth, xbc // 2), BF16),
+            pltpu.VMEM((xbc // 256, length + tail_rows, 256), F32),
+            pltpu.VMEM((n, HEADS, block), BF16),
+            dma((2, streams, n)), dma((2, streams, n)),
+            dma((2, n)), dma((2, n)), dma((2, n)), dma((2, n)),
+            dma((n,)), dma((n,)), dma((3,)), dma(()), dma(()),
+        ],
+        compiler_params=pltpu.CompilerParams(
+            collective_id=2, has_side_effects=True, vmem_limit_bytes=60 * 2**20
+        ),
+        name="project",
+    )(tokens, w_in, dt_block)
+
+
 def per_device(tokens, w_in, w_dt, conv_w, conv_b, dt_bias, a_log, d_skip, norm_gain):
     own_rows = tokens.reshape(tokens.shape[1], tokens.shape[2])
     row_count = own_rows.shape[0]
-    n_in, n_out = lax.axis_size("inner"), lax.axis_size("outer")
-    full_x = lax.all_gather(w_in, "inner", axis=0, tiled=True)
-    full_dt = lax.all_gather(w_dt, "inner", axis=0, tiled=True)
-    projected = jnp.dot(own_rows, full_x, preferred_element_type=F32).astype(BF16)
-    dt_raw = jnp.dot(own_rows, full_dt, preferred_element_type=F32).astype(BF16)
-    order = [(r, r + 1) for r in range(n_in * n_out - 1)]
-    pairs = [((r % n_in) * n_out + r // n_in, (s % n_in) * n_out + s // n_in) for r, s in order]
-    tail = lax.ppermute(projected[row_count - 8 :], ("inner", "outer"), pairs)
+    projected, tail, dt_raw = run_project(own_rows, w_in, w_dt)
     mixed, entry = run_scan(
         projected, tail, dt_raw, conv_w, conv_b, dt_bias, a_log, d_skip, norm_gain
     )

time: 267 us -> 118 us (0.44)
  waiting for transfers between devices: 154 us -> 0 us
  Pallas kernels: 42.4 us -> 111 us
  blocking collectives: 26.5 us -> 0 us
  matrix products: 19.2 us -> 0 us
  between operations: 14.1 us -> 0.66 us
    all_gather x1 -> x0, waiting for transfers between devices: 154 us -> none  [per_device(): full_x = lax.all_gather(w_in, 'inner', axis=0, tiled=True)]
    pallas_call x0 -> x1, Pallas kernels: none -> 65.7 us  [run_project(): pl.pallas_call(partial(project_kernel, n, n_out), out_shape=(jax.ShapeDty...]
    all_gather x1 -> x0, blocking collectives: 26.5 us -> none  [per_device(): full_dt = lax.all_gather(w_dt, 'inner', axis=0, tiled=True)]
    dot_general x2 -> x0, matrix products: 19.2 us -> none  [the longest x1 14.7 us: per_device(): jnp.dot(own_rows, full_x, preferred_element_type=F32).astype(BF16)]
    unnamed x10 -> x4, local copies, waits for them, and re-layouts: 5.58 us -> 3.73 us
  transfers between devices with their start and end apart: 2 -> 0, of which waited for: 1 -> 0; matrix products, arithmetic and copies ran while one was open for 3% -> 0% of each run, Pallas kernels for 0% -> 0%
where the time goes in v2:
time: 118 us
  Pallas kernels  111 us (94%)
  local copies, waits for them, and re-layouts  6.42 us (5%)
    pallas_call x1, Pallas kernels, run_project(): pl.pallas_call(partial(project_kernel, n, n_out), out_shape=(jax.ShapeDty...  65.7 us
    pallas_call x1, Pallas kernels, run_scan(): pl.pallas_call(partial(scan_kernel, n_in, ndev), out_shape=(jax.ShapeDtyp...  44.9 us
    unnamed x4, local copies, waits for them, and re-layouts  3.73 us

profile of v2, /device:TPU:1, one launch (start us, length us, event | category | flops | bytes accessed | tf_op | source)
XLA Modules:
  0.0 117.7 jit_solution(2428735015414186747)
XLA Ops:
  0.6 1.3 %broadcast_in_dim.15.conv_b = f32[1,1536]{1,0:T(1,128)} reshape(f32[1536]{0:T(1024)} %param.13) | data formatting | bytes 12288 | tf_op jit(solution)/shard_map/broadcast_in_dim | solution.py:268
  1.9 0.7 broadcast_in_dim.18
  2.6 0.7 broadcast_in_dim_reshape.3.d_skip
  3.3 65.7 %project.1 = (bf16[768,1536]{1,0:T(8,128)(2,1)}, bf16[16,1536]{1,0:T(8,128)(2,1)}, bf16[768,16]{1,0:T(8,128)(2,1)}) custom-call(bf16[768,4096]{1,0:T(8,128)(2,1)} %bitcast.7, bf16[512,1536]{1,0:T(8,128)(2,1)} %w_in.1, bf16[16,512]{1,0:T(8,128)(2,1)} %bitcast.10), custom_call_target="tpu_custom_call" | custom-call | tf_op jit(solution)/shard_map/project/pallas_call | solution.py:573
  69.0 44.9 %scan.1 = (bf16[768,1024]{1,0:T(8,128)(2,1)}, f32[1024,256]{1,0:T(8,128)}) custom-call(bf16[768,1536]{1,0:T(8,128)(2,1)} %get-tuple-element.7.proj, bf16[16,1536]{1,0:T(8,128)(2,1)} %get-tuple-element.8.tail, bf16[768,16]{1,0:T(8,128)(2,1)} %get-tuple-element.9.dt_raw, f32[4,1536]{1,0:T(4,128)} %conv_w.1, f32[1,1536]{1,0:T(1,128)} %broadcast_in_dim.15.conv_b, ...), custom_call_target="tpu_custom_call" | custom-call | tf_op jit(solution)/shard_map/scan/pallas_call | solution.py:239
  113.9 0.0 copy-start
  113.9 2.8 %copy.13 = bf16[1,768,1024]{2,1,0:T(8,128)(2,1)} copy(bf16[1,768,1024]{2,1,0:T(8,128)(2,1)} %bitcast.8) | data formatting | bytes 3145728
  116.7 0.0 copy-done
  116.7 1.0 copy.14
Async XLA Ops:
  113.9 2.8 %copy-start = (f32[1024,256]{1,0:T(8,128)S(1)}, f32[1024,256]{1,0:T(8,128)}, u32[]{:S(2)}) copy-start(f32[1024,256]{1,0:T(8,128)} %get-tuple-element.11) | copy-start | bytes 3145732

commit v3 on v2

--- a/solution.py
+++ b/solution.py
@@ -33,7 +33,7 @@
     n_in, ndev,
     proj, tail, dt_raw, conv_w, conv_b, dt_bias, a_log, d_skip, gain,
     mixed, entry_out,
-    pad, conv, log_s, log_t, step_s, y, states,
+    bias_row, skip_row, pad, conv, log_s, log_t, step_s, y, states,
     send1, recv1, send2, recv2, dec_send, dec_recv,
     ss1, rs1, ss2, rs2, ssd, rsd,
 ):
@@ -59,8 +59,15 @@
     col_head = lax.broadcasted_iota(jnp.int32, (HEADS, HP), 1) // P_SIZE
     spread = (head_id == col_head).astype(F32).astype(BF16)
 
-    step_size = jax.nn.softplus(dt_raw[...].astype(F32) + dt_bias[...])
-    scaled = step_size * (-jnp.exp(a_log[...]))
+    bias_row[...] = conv_b[...].reshape(1, conv_b.shape[0])
+    gain_row = gain[...].reshape(1, HP)
+    skip = d_skip[...].reshape(1, HEADS)
+    skip_high = skip.astype(BF16).astype(F32)
+    skip_row[...] = expand(skip - skip_high, spread) + jnp.dot(
+        skip_high.astype(BF16), spread, preferred_element_type=F32
+    )
+    step_size = jax.nn.softplus(dt_raw[...].astype(F32) + dt_bias[...].reshape(1, HEADS))
+    scaled = step_size * (-jnp.exp(a_log[...].reshape(1, HEADS)))
     row_id = lax.broadcasted_iota(jnp.int32, (CHUNK, CHUNK), 0)
     col_id = lax.broadcasted_iota(jnp.int32, (CHUNK, CHUNK), 1)
     causal = col_id <= row_id
@@ -88,7 +95,7 @@
         i, j = lax.div(t, blocks), lax.rem(t, blocks)
         cols = pl.ds(pl.multiple_of(j * wide, wide), wide)
         window = pad[pl.ds(pl.multiple_of(i * 128, 128), 136), cols]
-        total = conv_b[:, cols]
+        total = bias_row[:, cols]
         for k in range(CONV):
             total = total + conv_w[k : k + 1, cols] * window[5 + k : 5 + k + 128]
         conv[pl.ds(pl.multiple_of(i * 128, 128), 128), cols] = (
@@ -155,7 +162,7 @@
         x_rows = conv[here, 0:HP].astype(F32)
         driven = (expand(step_s[here], spread) * x_rows).astype(BF16)
         inter = lax.dot_general(c_rows, states[c], LAST, preferred_element_type=F32)
-        y[here] = expand(jnp.exp(log_c - reached), spread) * inter + d_skip[...] * x_rows
+        y[here] = expand(jnp.exp(log_c - reached), spread) * inter + skip_row[...] * x_rows
         for h in range(0, HEADS, 2):
             pieces = []
             for k in (h, h + 1):
@@ -226,7 +233,7 @@
         sums = lax.dot_general(high, spread, LAST, preferred_element_type=F32)
         sums = sums + lax.dot_general(low, spread, LAST, preferred_element_type=F32)
         inv_rms = lax.rsqrt(sums * (1.0 / P_SIZE) + EPSILON)
-        mixed[here] = (out * expand(inv_rms, spread) * gain[...]).astype(BF16)
+        mixed[here] = (out * expand(inv_rms, spread) * gain_row).astype(BF16)
 
 
 def run_scan(projected, tail, dt_raw, conv_w, conv_b, dt_bias, a_log, d_skip, norm_gain):
@@ -245,6 +252,8 @@
         in_specs=[vmem] * 9,
         out_specs=(vmem, vmem),
         scratch_shapes=[
+            pltpu.VMEM((1, xbc), F32),
+            pltpu.VMEM((1, HP), F32),
             pltpu.VMEM((length + 8, xbc), F32),
             pltpu.VMEM((length, xbc), BF16),
             pltpu.VMEM((length, HEADS), F32),
@@ -265,8 +274,7 @@
         ),
         name="scan",
     )(
-        projected, tail, dt_raw, conv_w, conv_b[None, :], dt_bias[None, :], a_log[None, :],
-        jnp.repeat(d_skip, P_SIZE)[None, :], norm_gain[None, :],
+        projected, tail, dt_raw, conv_w, conv_b, dt_bias, a_log, d_skip, norm_gain,
     )
 
 
@@ -348,54 +356,48 @@
     def owner_of(d, s):
         return index_at(pos - s) if d == 0 else index_at(pos + s)
 
-    def side_copy(d, s):
-        rows = pl.ds(
-            pl.multiple_of(owner_of(d, s) * local + grp * ring_rows, 16), third
-        )
-        cols = pl.ds(pl.multiple_of(core * quarter, lanes), quarter)
-        part = held.at[d, rows, cols]
-        return pltpu.make_async_remote_copy(
-            src_ref=part, dst_ref=part, send_sem=side_s.at[d, s],
-            recv_sem=side_r.at[d, s], device_id={"grp": 1 - grp}, device_id_type=MESH,
-        )
-
-    def core_copy(d, s):
-        cols = pl.ds(pl.multiple_of(core * quarter, lanes), quarter)
-        part = held.at[d, own_rows(owner_of(d, s)), cols]
-        return pltpu.make_async_remote_copy(
-            src_ref=part, dst_ref=part, send_sem=core_s.at[d, s],
-            recv_sem=core_r.at[d, s], device_id={"outer": 1 - core}, device_id_type=MESH,
-        )
+    def chunk_cols(which, t):
+        return pl.ds(pl.multiple_of(which * quarter + t * lanes, lanes), lanes)
+
+    def side_rows(d, s, which):
+        start = owner_of(d, s) * local + which * ring_rows
+        return pl.ds(pl.multiple_of(start, 16), third)
+
+    def side_between(d, t, s, which):
+        part = held.at[d, side_rows(d, s, which), chunk_cols(core, t)]
+        return pltpu.make_async_remote_copy(
+            src_ref=part, dst_ref=part, send_sem=side_s.at[d, t, s],
+            recv_sem=side_r.at[d, t, s], device_id={"grp": 1 - grp}, device_id_type=MESH,
+        )
+
+    def core_between(d, t, s, which):
+        part = held.at[d, own_rows(owner_of(d, s)), chunk_cols(which, t)]
+        return pltpu.make_async_remote_copy(
+            src_ref=part, dst_ref=part, send_sem=core_s.at[d, t, s],
+            recv_sem=core_r.at[d, t, s], device_id={"outer": 1 - core}, device_id_type=MESH,
+        )
+
+    def side_copy(d, t, s):
+        return side_between(d, t, s, grp)
+
+    def core_copy(d, t, s):
+        return core_between(d, t, s, core)
 
     def ring_arrival(d, t, s):
-        owner = owner_of(d, s)
-        rows = pl.ds(pl.multiple_of(owner * local + grp * third, 16), ring_rows)
-        cols = pl.ds(pl.multiple_of(core * quarter + t * lanes, lanes), lanes)
-        part = held.at[d, rows, cols]
+        start = owner_of(d, s) * local + grp * third
+        rows = pl.ds(pl.multiple_of(start, 16), ring_rows)
+        part = held.at[d, rows, chunk_cols(core, t)]
         pltpu.make_async_remote_copy(
             src_ref=part, dst_ref=part, send_sem=ring_s.at[d, t, s],
             recv_sem=ring_r.at[d, t, s], device_id={"inner": index_at(pos + 1)},
             device_id_type=MESH,
         ).wait_recv()
 
-    def side_arrival(d, s):
-        rows = pl.ds(
-            pl.multiple_of(owner_of(d, s) * local + (1 - grp) * ring_rows, 16), third
-        )
-        cols = pl.ds(pl.multiple_of(core * quarter, lanes), quarter)
-        part = held.at[d, rows, cols]
-        pltpu.make_async_remote_copy(
-            src_ref=part, dst_ref=part, send_sem=side_s.at[d, s],
-            recv_sem=side_r.at[d, s], device_id={"grp": 1 - grp}, device_id_type=MESH,
-        ).wait_recv()
-
-    def core_arrival(d, s):
-        cols = pl.ds(pl.multiple_of((1 - core) * quarter, lanes), quarter)
-        part = held.at[d, own_rows(owner_of(d, s)), cols]
-        pltpu.make_async_remote_copy(
-            src_ref=part, dst_ref=part, send_sem=core_s.at[d, s],
-            recv_sem=core_r.at[d, s], device_id={"outer": 1 - core}, device_id_type=MESH,
-        ).wait_recv()
+    def side_arrival(d, t, s):
+        side_between(d, t, s, 1 - grp).wait_recv()
+
+    def core_arrival(d, t, s):
+        core_between(d, t, s, 1 - core).wait_recv()
 
     def dt_copy(k):
         peer = lax.rem(me + k, n)
@@ -442,17 +444,20 @@
 
     incremental = local % 128 == 0
 
+    def multiply_tile(d, lhs_cols, rhs_rows, first, j):
+        cols = pl.ds(pl.multiple_of(j * wide, wide), wide)
+        product = jnp.dot(
+            tok[:, lhs_cols], held[d, rhs_rows, cols], preferred_element_type=F32
+        )
+        at = d * tiles + j
+        if first:
+            total[at] = product
+        else:
+            total[at] = total[at] + product
+
     def multiply(d, lhs_cols, rhs_rows, first):
         def tile(j, carry):
-            cols = pl.ds(pl.multiple_of(j * wide, wide), wide)
-            product = jnp.dot(
-                tok[:, lhs_cols], held[d, rhs_rows, cols], preferred_element_type=F32
-            )
-            at = d * tiles + j
-            if first:
-                total[at] = product
-            else:
-                total[at] = total[at] + product
+            multiply_tile(d, lhs_cols, rhs_rows, first, j)
             return carry
 
         lax.fori_loop(0, tiles, tile, 0)
@@ -478,46 +483,50 @@
         dt_out[...] = sums.astype(BF16)
 
     def step(s, carry):
-        @pl.when(s < n)
+        @pl.when(s >= 3)
         def _():
             for t in range(streams):
                 for d in range(2):
+                    core_arrival(d, t, s - 2)
+
+        def part(t, inner):
+            @pl.when(s < n)
+            def _():
+                for d in range(2):
                     ring_arrival(d, t, s)
 
                     @pl.when(s < n - 1)
                     def _():
                         ring_copy(d, t, s + 1).start()
 
-            for d in range(2):
-                side_copy(d, s).start()
-
-        @pl.when((s >= 2) & (s <= n))
-        def _():
-            for d in range(2):
-                side_arrival(d, s - 1)
-                core_copy(d, s - 1).start()
-
-        @pl.when(s >= 3)
-        def _():
-            for d in range(2):
-                core_arrival(d, s - 2)
+                    side_copy(d, t, s).start()
+
+            @pl.when((s >= 2) & (s <= n))
+            def _():
+                for d in range(2):
+                    side_arrival(d, t, s - 1)
+                    core_copy(d, t, s - 1).start()
+
+            if incremental:
+                for d in range(2):
+                    owner = owner_of(d, s - 2)
+                    at = pl.ds(pl.multiple_of(owner * local, 128), local)
+
+                    @pl.when(s == 2)
+                    def _():
+                        multiply_tile(d, at, at, True, t)
+
+                    @pl.when(s > 2)
+                    def _():
+                        multiply_tile(d, at, at, False, t)
+
+            return inner
+
+        lax.fori_loop(0, streams, part, 0)
 
         @pl.when(s == 1)
         def _():
             project_dt()
-
-        if incremental:
-            for d in range(2):
-                owner = owner_of(d, s - 2)
-                at = pl.ds(pl.multiple_of(owner * local, 128), local)
-
-                @pl.when(s == 2)
-                def _():
-                    multiply(d, at, at, True)
-
-                @pl.when(s > 2)
-                def _():
-                    multiply(d, at, at, False)
 
         return carry
 
@@ -542,8 +551,8 @@
         for d in range(2):
             for t in range(streams):
                 ring_copy(d, t, s).wait_send()
-            side_copy(d, s).wait_send()
-            core_copy(d, s).wait_send()
+                side_copy(d, t, s).wait_send()
+                core_copy(d, t, s).wait_send()
         dt_copy(s).wait_send()
         return carry
 
@@ -585,7 +594,8 @@
             pltpu.VMEM((xbc // 256, length + tail_rows, 256), F32),
             pltpu.VMEM((n, HEADS, block), BF16),
             dma((2, streams, n)), dma((2, streams, n)),
-            dma((2, n)), dma((2, n)), dma((2, n)), dma((2, n)),
+            dma((2, streams, n)), dma((2, streams, n)),
+            dma((2, streams, n)), dma((2, streams, n)),
             dma((n,)), dma((n,)), dma((3,)), dma(()), dma(()),
         ],
         compiler_params=pltpu.CompilerParams(

time: 118 us -> 113 us (0.958)
  local copies, waits for them, and re-layouts: 6.42 us -> 3.73 us
  Pallas kernels: 111 us -> 109 us
    broadcast_in_dim x2 -> x0, local copies, waits for them, and re-layouts: 2.02 us -> none  [the longest x1 1.3 us: run_scan(): conv_b[None, :]]
    pallas_call x1, Pallas kernels: 65.7 us -> 64.1 us  [run_project(): pl.pallas_call(partial(project_kernel, n, n_out), out_shape=(jax.ShapeDty...]
where the time goes in v3:
time: 113 us
  Pallas kernels  109 us (96%)
  local copies, waits for them, and re-layouts  3.73 us (3%)
    pallas_call x1, Pallas kernels, run_project(): pl.pallas_call(partial(project_kernel, n, n_out), out_shape=(jax.ShapeDty...  64.1 us
    pallas_call x1, Pallas kernels, run_scan(): pl.pallas_call(partial(scan_kernel, n_in, ndev), out_shape=(jax.ShapeDtyp...  44.4 us
    unnamed x4, local copies, waits for them, and re-layouts  3.73 us

profile of v3, /device:TPU:1, one launch (start us, length us, event | category | flops | bytes accessed | tf_op | source)
XLA Modules:
  0.0 112.9 jit_solution(4491907069347881767)
XLA Ops:
  0.6 64.1 %project.1 = (bf16[768,1536]{1,0:T(8,128)(2,1)}, bf16[16,1536]{1,0:T(8,128)(2,1)}, bf16[768,16]{1,0:T(8,128)(2,1)}) custom-call(bf16[768,4096]{1,0:T(8,128)(2,1)} %bitcast.4, bf16[512,1536]{1,0:T(8,128)(2,1)} %w_in.1, bf16[16,512]{1,0:T(8,128)(2,1)} %bitcast.7), custom_call_target="tpu_custom_call" | custom-call | tf_op jit(solution)/shard_map/project/pallas_call | solution.py:582
  64.8 44.4 %scan.1 = (bf16[768,1024]{1,0:T(8,128)(2,1)}, f32[1024,256]{1,0:T(8,128)}) custom-call(bf16[768,1536]{1,0:T(8,128)(2,1)} %get-tuple-element.7.proj, bf16[16,1536]{1,0:T(8,128)(2,1)} %get-tuple-element.8.tail, bf16[768,16]{1,0:T(8,128)(2,1)} %get-tuple-element.9.dt_raw, f32[4,1536]{1,0:T(4,128)} %conv_w.1, f32[1536]{0:T(1024)} %conv_b.1, f32[16]{0:T(128)} %dt_bias.1, ...), custom_call_target="tpu_custom_call" | custom-call | tf_op jit(solution)/shard_map/scan/pallas_call | solution.py:246
  109.2 0.0 copy-start
  109.2 2.8 %copy.13 = bf16[1,768,1024]{2,1,0:T(8,128)(2,1)} copy(bf16[1,768,1024]{2,1,0:T(8,128)(2,1)} %bitcast.5) | data formatting | bytes 3145728
  111.9 0.0 copy-done
  111.9 1.0 copy.14
Async XLA Ops:
  109.2 2.8 %copy-start = (f32[1024,256]{1,0:T(8,128)S(1)}, f32[1024,256]{1,0:T(8,128)}, u32[]{:S(2)}) copy-start(f32[1024,256]{1,0:T(8,128)} %get-tuple-element.11) | copy-start | bytes 3145732

commit v4 on v3

--- a/solution.py
+++ b/solution.py
@@ -33,7 +33,7 @@
     n_in, ndev,
     proj, tail, dt_raw, conv_w, conv_b, dt_bias, a_log, d_skip, gain,
     mixed, entry_out,
-    bias_row, skip_row, pad, conv, log_s, log_t, step_s, y, states,
+    gain_s, bias_row, skip_row, pad, conv, log_s, log_t, step_s, y, states,
     send1, recv1, send2, recv2, dec_send, dec_recv,
     ss1, rs1, ss2, rs2, ssd, rsd,
 ):
@@ -60,7 +60,7 @@
     spread = (head_id == col_head).astype(F32).astype(BF16)
 
     bias_row[...] = conv_b[...].reshape(1, conv_b.shape[0])
-    gain_row = gain[...].reshape(1, HP)
+    gain_s[...] = gain[...].reshape(1, HP)
     skip = d_skip[...].reshape(1, HEADS)
     skip_high = skip.astype(BF16).astype(F32)
     skip_row[...] = expand(skip - skip_high, spread) + jnp.dot(
@@ -103,7 +103,15 @@
         ).astype(BF16)
         return carry
 
-    lax.fori_loop(0, (length // 128) * blocks, conv_block, 0)
+    row_blocks = length // 128
+
+    def conv_column(j):
+        def one(i, carry):
+            return conv_block(i * blocks + j, carry)
+
+        lax.fori_loop(0, row_blocks, one, 0)
+
+    conv_column(HP // wide)
 
     def weighted_sum(stop):
         final = log_s[stop - 1 : stop]
@@ -113,8 +121,6 @@
             weighted, conv[0:stop, HP : HP + N], FIRST, preferred_element_type=F32
         )
 
-    send1[...] = weighted_sum(length).reshape(ndev, rows, N).astype(BF16)
-    recv1[me] = send1[me]
     dec_recv[me] = dec_send[...]
 
     def decay_copy(g):
@@ -137,13 +143,46 @@
 
     pl.semaphore_wait(barrier, ndev - 1)
 
-    def send_first(k, carry):
-        g = lax.rem(me + k, ndev)
-        decay_copy(g).start()
-        first_copy(g).start()
-        return carry
-
-    lax.fori_loop(1, ndev, send_first, 0)
+    def send_decay(k, carry):
+        decay_copy(lax.rem(me + k, ndev)).start()
+        return carry
+
+    lax.fori_loop(1, ndev, send_decay, 0)
+
+    groups = HP // wide
+    owners = ndev // groups
+    own_group = lax.div(me, owners)
+    factor = jnp.exp(log_s[length - 1 : length] - log_s[...]) * step_s[...]
+
+    def spread_of(j):
+        head = lax.broadcasted_iota(jnp.int32, (HEADS, wide), 0)
+        col = lax.broadcasted_iota(jnp.int32, (HEADS, wide), 1) // P_SIZE
+        return (head == col + j * (wide // P_SIZE)).astype(F32).astype(BF16)
+
+    def first_group(i, carry):
+        j = lax.rem(own_group + 1 + i, groups)
+        conv_column(j)
+        cols = pl.ds(pl.multiple_of(j * wide, wide), wide)
+        weighted = (expand(factor, spread_of(j)) * conv[:, cols].astype(F32)).astype(BF16)
+        part = lax.dot_general(
+            weighted, conv[:, HP : HP + N], FIRST, preferred_element_type=F32
+        )
+        send1[pl.ds(j * owners, owners)] = part.reshape(owners, rows, N).astype(BF16)
+
+        def send_one(k, inner):
+            g = j * owners + k
+
+            @pl.when(g != me)
+            def _():
+                first_copy(g).start()
+
+            return inner
+
+        return lax.fori_loop(0, owners, send_one, carry)
+
+    lax.fori_loop(0, groups, first_group, 0)
+    recv1[me] = send1[me]
+    conv_column(HP // wide + 1)
 
     states[0] = jnp.zeros((HP, N), BF16)
     for c in range(1, chunks):
@@ -197,7 +236,6 @@
 
         @pl.when(r != me)
         def _():
-            second_copy(r).start()
             arrive(dec_recv, rsd, r)
             arrive(recv1, rs1, r)
 
@@ -206,34 +244,56 @@
         return decay * state + recv1[r].astype(F32)
 
     lax.fori_loop(0, ndev, advance, jnp.zeros((rows, N), F32))
+
+    def send_second(k, carry):
+        second_copy(lax.rem(me + k, ndev)).start()
+        return carry
+
+    lax.fori_loop(1, ndev, send_second, 0)
     recv2[me] = send2[me]
+
+    reach = jnp.exp(log_s[...])
+
+    def last_group(i, carry):
+        j = lax.rem(own_group + groups - 1 - i, groups)
+
+        def wait_one(k, inner):
+            g = j * owners + k
+
+            @pl.when(g != me)
+            def _():
+                arrive(recv2, rs2, g)
+
+            return inner
+
+        lax.fori_loop(0, owners, wait_one, 0)
+        cols = pl.ds(pl.multiple_of(j * wide, wide), wide)
+        entry = recv2[pl.ds(j * owners, owners)].astype(F32).reshape(wide, N)
+        entry_out[cols] = entry
+        carried = lax.dot_general(
+            conv[:, HP + N :], entry.astype(BF16), LAST, preferred_element_type=F32
+        )
+        spread_j = spread_of(j)
+        out = y[:, cols] + expand(reach, spread_j) * carried
+        square = out * out
+        high = square.astype(BF16)
+        low = (square - high.astype(F32)).astype(BF16)
+        sums = lax.dot_general(high, spread_j, LAST, preferred_element_type=F32)
+        sums = sums + lax.dot_general(low, spread_j, LAST, preferred_element_type=F32)
+        inv_rms = lax.rsqrt(sums * (1.0 / P_SIZE) + EPSILON)
+        mixed[:, cols] = (out * expand(inv_rms, spread_j) * gain_s[:, cols]).astype(BF16)
+        return carry
+
+    lax.fori_loop(0, groups, last_group, 0)
 
     def finish(k, carry):
         g = lax.rem(me + k, ndev)
-        arrive(recv2, rs2, g)
         decay_copy(g).wait_send()
         first_copy(g).wait_send()
         second_copy(g).wait_send()
         return carry
 
     lax.fori_loop(1, ndev, finish, 0)
-
-    entry = recv2[...].astype(F32).reshape(HP, N)
-    entry_out[...] = entry
-    entry = entry.astype(BF16)
-    for c in range(chunks):
-        here = slice(c * CHUNK, (c + 1) * CHUNK)
-        carried = lax.dot_general(
-            conv[here, HP + N :], entry, LAST, preferred_element_type=F32
-        )
-        out = y[here] + expand(jnp.exp(log_s[here]), spread) * carried
-        square = out * out
-        high = square.astype(BF16)
-        low = (square - high.astype(F32)).astype(BF16)
-        sums = lax.dot_general(high, spread, LAST, preferred_element_type=F32)
-        sums = sums + lax.dot_general(low, spread, LAST, preferred_element_type=F32)
-        inv_rms = lax.rsqrt(sums * (1.0 / P_SIZE) + EPSILON)
-        mixed[here] = (out * expand(inv_rms, spread) * gain_row).astype(BF16)
 
 
 def run_scan(projected, tail, dt_raw, conv_w, conv_b, dt_bias, a_log, d_skip, norm_gain):
@@ -252,6 +312,7 @@
         in_specs=[vmem] * 9,
         out_specs=(vmem, vmem),
         scratch_shapes=[
+            pltpu.VMEM((1, HP), F32),
             pltpu.VMEM((1, xbc), F32),
             pltpu.VMEM((1, HP), F32),
             pltpu.VMEM((length + 8, xbc), F32),

time: 113 us -> 107 us (0.947)
  the two profiles are of different devices: /device:TPU:1 before, /device:TPU:0 now
where the time goes in v4:
time: 107 us
  Pallas kernels  102 us (95%)
  local copies, waits for them, and re-layouts  3.73 us (3%)
    pallas_call x1, Pallas kernels, run_project(): pl.pallas_call(partial(project_kernel, n, n_out), out_shape=(jax.ShapeDty...  64 us
    pallas_call x1, Pallas kernels, run_scan(): pl.pallas_call(partial(scan_kernel, n_in, ndev), out_shape=(jax.ShapeDtyp...  38.3 us
    unnamed x4, local copies, waits for them, and re-layouts  3.73 us

profile of v4, /device:TPU:0, one launch (start us, length us, event | category | flops | bytes accessed | tf_op | source)
XLA Modules:
  0.0 106.6 jit_solution(15669389267056945779)
XLA Ops:
  0.6 64.0 %project.1 = (bf16[768,1536]{1,0:T(8,128)(2,1)}, bf16[16,1536]{1,0:T(8,128)(2,1)}, bf16[768,16]{1,0:T(8,128)(2,1)}) custom-call(bf16[768,4096]{1,0:T(8,128)(2,1)} %bitcast.4, bf16[512,1536]{1,0:T(8,128)(2,1)} %w_in.1, bf16[16,512]{1,0:T(8,128)(2,1)} %bitcast.7), custom_call_target="tpu_custom_call" | custom-call | tf_op jit(solution)/shard_map/project/pallas_call | solution.py:643
  64.6 38.3 %scan.1 = (bf16[768,1024]{1,0:T(8,128)(2,1)}, f32[1024,256]{1,0:T(8,128)}) custom-call(bf16[768,1536]{1,0:T(8,128)(2,1)} %get-tuple-element.7.proj, bf16[16,1536]{1,0:T(8,128)(2,1)} %get-tuple-element.8.tail, bf16[768,16]{1,0:T(8,128)(2,1)} %get-tuple-element.9.dt_raw, f32[4,1536]{1,0:T(4,128)} %conv_w.1, f32[1536]{0:T(1024)} %conv_b.1, f32[16]{0:T(128)} %dt_bias.1, ...), custom_call_target="tpu_custom_call" | custom-call | tf_op jit(solution)/shard_map/scan/pallas_call | solution.py:306
  102.9 0.0 copy-start
  102.9 2.8 %copy.13 = bf16[1,768,1024]{2,1,0:T(8,128)(2,1)} copy(bf16[1,768,1024]{2,1,0:T(8,128)(2,1)} %bitcast.5) | data formatting | bytes 3145728
  105.6 0.0 copy-done
  105.6 1.0 copy.14
Async XLA Ops:
  102.9 2.8 %copy-start = (f32[1024,256]{1,0:T(8,128)S(1)}, f32[1024,256]{1,0:T(8,128)}, u32[]{:S(2)}) copy-start(f32[1024,256]{1,0:T(8,128)} %get-tuple-element.11) | copy-start | bytes 3145732
